TPU v7x, 32 devices: a whole 2x2x4 slice. The times are simulated.
32 devices in a mesh: dp: 8 (over z, y), tensor: 4 (over x, core).
Axes of the slice: x: 2, y: 2, z: 4, core: 2. Of those that a mesh axis runs over, the one named last changes fastest.
Arguments:
- tokens: bfloat16 [8192, 1024], P(('dp', 'tensor')), may hold values from -6 to 6
- cotangent: float32 [8192, 1024], P(('dp', 'tensor')), may hold values from -6 to 6
- lengths: int32 [8, 2], P('dp'), may hold values from 64 to 512, as said below
- order: int32 [8, 1024], P('dp'), may hold values from 0 to 1023, each once within a row
- adapter_ids: int32 [8, 2], P('dp'), may hold values from 0 to 7
- norm1_gain: float32 [1024], replicated, may hold values from 0.25 to 1.75
- norm1_shift: float32 [1024], replicated, may hold values from -1.5 to 1.5
- qkv_weight: bfloat16 [1024, 3, 1024], P(None, None, 'tensor'), may hold values from -0.1875 to 0.1875
- qv_bias: float32 [2, 1024], P(None, 'tensor'), may hold values from -1.5 to 1.5
- proj_weight: bfloat16 [1024, 1024], P('tensor'), may hold values from -1.5 to 1.5
- proj_bias: float32 [1024], replicated, may hold values from -1.5 to 1.5
- norm2_gain: float32 [1024], replicated, may hold values from 0.25 to 1.75
- norm2_shift: float32 [1024], replicated, may hold values from -1.5 to 1.5
- up_weight: bfloat16 [1024, 4096], P(None, 'tensor'), may hold values from -0.1875 to 0.1875
- up_bias: float32 [4096], P('tensor'), may hold values from -1.5 to 1.5
- down_weight: bfloat16 [4096, 1024], P('tensor'), may hold values from -0.09375 to 0.09375
- down_bias: float32 [1024], replicated, may hold values from -1.5 to 1.5
- adapt_qkv_in: bfloat16 [1024, 128], replicated, may hold values from -0.1875 to 0.1875
- adapt_qkv_out: bfloat16 [128, 3, 1024], P(None, None, 'tensor'), may hold values from -0.75 to 0.75
- adapt_proj_in: bfloat16 [1024, 128], P('tensor'), may hold values from -0.75 to 0.75
- adapt_proj_out: bfloat16 [128, 1024], replicated, may hold values from -0.75 to 0.75
- adapt_up_in: bfloat16 [1024, 128], replicated, may hold values from -0.1875 to 0.1875
- adapt_up_out: bfloat16 [128, 4096], P(None, 'tensor'), may hold values from -0.75 to 0.75
- adapt_down_in: bfloat16 [4096, 128], P('tensor'), may hold values from -0.09375 to 0.09375
- adapt_down_out: bfloat16 [128, 1024], replicated, may hold values from -0.75 to 0.75
Outputs:
- result: float32 [8192, 1024], P(('dp', 'tensor'))
- grad_input: float32 [8192, 1024], P(('dp', 'tensor'))
- grad_qkv_in: float32 [1024, 128], replicated
- grad_qkv_out: float32 [128, 3, 1024], P(None, None, 'tensor')
- grad_proj_in: float32 [1024, 128], P('tensor')
- grad_proj_out: float32 [128, 1024], replicated
- grad_up_in: float32 [1024, 128], replicated
- grad_up_out: float32 [128, 4096], P(None, 'tensor')
- grad_down_in: float32 [4096, 128], P('tensor')
- grad_down_out: float32 [128, 1024], replicated
Inputs may be any that keep to these rules, and one draw needn't show every extreme that they name: `lengths`: in every group one sequence has exactly 512 valid tokens; the others have at least 512 // 8 (and at least one). `order`: each row is a permutation of the group's 1024 stored rows.
All inputs are finite; a program needn't handle non-finite values.
Results may differ from a plain program's by a relative error of at most 0.023.
Values may be sent and summed in bfloat16 or wider, within the bound.
No kernel may reach another device: no remote copies, remote signals or barrier semaphores. Data moves between devices by JAX's collectives and lax.ppermute only.
A program may use at most 128 MiB of HBM per device.

v0:
```python
import math
import jax
import jax.numpy as jnp
from jax import lax
from jax.sharding import PartitionSpec as P

D = 1024
HD = 64
RANK = 16
EPSILON = 1e-05
NEGATIVE = -1000000000.0


def layer_norm(values, gain, shift):
    centre = values - jnp.mean(values, -1, keepdims=True)
    spread = jnp.mean(centre * centre, -1, keepdims=True)
    return centre * lax.rsqrt(spread + EPSILON) * gain + shift


def matmul(left, right):
    return jnp.dot(left, right, preferred_element_type=jnp.float32)


def matmul_back(left, right):
    return lax.dot_general(
        left, right, (((1,), (1,)), ((), ())), preferred_element_type=jnp.float32
    )


def matmul_over(left, right):
    return lax.dot_general(
        left, right, (((0,), (0,)), ((), ())), preferred_element_type=jnp.float32
    )


def gelu_tanh(values):
    return jax.nn.gelu(values, approximate=True)


def block_scores(queries, keys, query_start, length):
    scale = 1.0 / math.sqrt(HD)
    scores = jnp.einsum("qhc,khc->hqk", queries, keys, preferred_element_type=jnp.float32) * scale
    query_pos = query_start + jnp.arange(queries.shape[0], dtype=jnp.int32)
    key_pos = jnp.arange(keys.shape[0], dtype=jnp.int32)
    allowed = (key_pos[None, :] <= query_pos[:, None]) & (key_pos[None, :] < length)
    return jnp.where(allowed[None], scores, NEGATIVE)


def attention_forward(qkv_seq, lengths_row, seq_len):
    group_rows = qkv_seq.shape[0]
    heads_here = qkv_seq.shape[2] // HD
    block_rows = min(512, seq_len)
    per_seq = seq_len // block_rows
    split = qkv_seq.reshape(group_rows, 3, heads_here, HD)

    def one_block(block_id):
        seq_id = block_id // per_seq
        query_start = block_id % per_seq * block_rows
        base = seq_id * seq_len
        queries = lax.dynamic_slice_in_dim(split[:, 0], base + query_start, block_rows, 0)
        keys = lax.dynamic_slice_in_dim(split[:, 1], base, seq_len, 0)
        values = lax.dynamic_slice_in_dim(split[:, 2], base, seq_len, 0)
        scores = block_scores(queries, keys, query_start, lengths_row[seq_id])
        top = jnp.max(scores, -1, keepdims=True)
        weights = jnp.exp(scores - top)
        total = jnp.sum(weights, -1, keepdims=True)
        probs = (weights / total).astype(jnp.bfloat16)
        attended = jnp.einsum("hqk,khc->qhc", probs, values, preferred_element_type=jnp.float32)
        return (attended.reshape(block_rows, heads_here * HD), (top + jnp.log(total))[..., 0])

    blocks = group_rows // block_rows
    outputs, log_totals = lax.map(one_block, jnp.arange(blocks, dtype=jnp.int32))
    return (outputs.reshape(group_rows, heads_here * HD), log_totals)


def attention_backward(qkv_seq, grad_seq, log_totals, lengths_row, seq_len):
    group_rows = qkv_seq.shape[0]
    heads_here = qkv_seq.shape[2] // HD
    block_rows = min(512, seq_len)
    per_seq = seq_len // block_rows
    seqs = group_rows // seq_len
    scale = 1.0 / math.sqrt(HD)
    split = qkv_seq.reshape(group_rows, 3, heads_here, HD)
    grad_split = grad_seq.reshape(group_rows, heads_here, HD)

    def one_block(block_id):
        seq_id = block_id // per_seq
        query_start = block_id % per_seq * block_rows
        base = seq_id * seq_len
        queries = lax.dynamic_slice_in_dim(split[:, 0], base + query_start, block_rows, 0)
        keys = lax.dynamic_slice_in_dim(split[:, 1], base, seq_len, 0)
        values = lax.dynamic_slice_in_dim(split[:, 2], base, seq_len, 0)
        grad_block = lax.dynamic_slice_in_dim(grad_split, base + query_start, block_rows, 0)
        scores = block_scores(queries, keys, query_start, lengths_row[seq_id])
        probs = jnp.exp(scores - log_totals[block_id][..., None])
        grad_probs = jnp.einsum(
            "qhc,khc->hqk", grad_block, values, preferred_element_type=jnp.float32
        )
        centre = jnp.sum(probs * grad_probs, -1, keepdims=True)
        grad_raw = (probs * (grad_probs - centre) * scale).astype(jnp.bfloat16)
        grad_query = jnp.einsum("hqk,khc->qhc", grad_raw, keys, preferred_element_type=jnp.float32)
        grad_key = jnp.einsum("hqk,qhc->khc", grad_raw, queries, preferred_element_type=jnp.float32)
        grad_value = jnp.einsum(
            "hqk,qhc->khc",
            probs.astype(jnp.bfloat16),
            grad_block,
            preferred_element_type=jnp.float32,
        )
        return (grad_query, grad_key, grad_value)

    blocks = group_rows // block_rows
    grad_query, grad_key, grad_value = lax.map(one_block, jnp.arange(blocks, dtype=jnp.int32))
    width_here = heads_here * HD
    grad_query = grad_query.reshape(group_rows, width_here)
    grad_key = jnp.sum(grad_key.reshape(seqs, per_seq, seq_len, width_here), axis=1).reshape(
        group_rows, width_here
    )
    grad_value = jnp.sum(grad_value.reshape(seqs, per_seq, seq_len, width_here), axis=1).reshape(
        group_rows, width_here
    )
    return jnp.stack([grad_query, grad_key, grad_value], 1)


def body(
    tokens,
    cotangent,
    lengths,
    order,
    adapter_ids,
    norm1_gain,
    norm1_shift,
    qkv_weight,
    qv_bias,
    proj_weight,
    proj_bias,
    norm2_gain,
    norm2_shift,
    up_weight,
    up_bias,
    down_weight,
    down_bias,
    adapt_qkv_in,
    adapt_qkv_out,
    adapt_proj_in,
    adapt_proj_out,
    adapt_up_in,
    adapt_up_out,
    adapt_down_in,
    adapt_down_out,
):
    own_rows = tokens.shape[0]
    order_row = order[0]
    lengths_row = lengths[0]
    ids_row = adapter_ids[0]
    group_rows = order_row.shape[0]
    seqs = lengths_row.shape[0]
    seq_len = group_rows // seqs
    adapt_cols = adapt_qkv_in.shape[1]
    rank_index = lax.axis_index("tensor")
    inverse = (
        jnp.zeros((group_rows,), jnp.int32)
        .at[order_row]
        .set(jnp.arange(group_rows, dtype=jnp.int32))
    )
    seq_of = inverse // seq_len
    adapter_of = jnp.sum(
        jnp.where(
            seq_of[:, None] == jnp.arange(seqs, dtype=jnp.int32)[None, :], ids_row[None, :], 0
        ),
        axis=1,
    )
    group_mask = (
        jnp.arange(adapt_cols, dtype=jnp.int32)[None, :] // RANK == adapter_of[:, None]
    ).astype(jnp.float32)
    own_mask = lax.dynamic_slice_in_dim(group_mask, rank_index * own_rows, own_rows, 0)
    bias_three = jnp.stack([qv_bias[0], jnp.zeros_like(qv_bias[0]), qv_bias[1]])
    proj_joined = jnp.concatenate([proj_weight, adapt_proj_in], 1)
    down_joined = jnp.concatenate([down_weight, adapt_down_in], 1)
    up_joined = jnp.concatenate([up_weight, adapt_up_out], 0)
    qkv_joined = jnp.concatenate([qkv_weight, adapt_qkv_out], 0)

    def project_qkv(rows_all, lowrank_all):
        value = jnp.einsum("rd,dkc->rkc", rows_all, qkv_weight, preferred_element_type=jnp.float32)
        value = value + jnp.einsum(
            "ra,akc->rkc", lowrank_all, adapt_qkv_out, preferred_element_type=jnp.float32
        )
        return (value + bias_three[None]).astype(jnp.bfloat16)

    def project_up(rows_all, lowrank_all):
        return matmul(rows_all, up_weight) + matmul(lowrank_all, adapt_up_out) + up_bias

    inputs = tokens.astype(jnp.float32)
    normed1 = layer_norm(inputs, norm1_gain, norm1_shift).astype(jnp.bfloat16)
    low1 = (matmul(normed1, adapt_qkv_in) * own_mask).astype(jnp.bfloat16)
    normed1_all, low1_small = (
        lax.all_gather(normed1, "tensor", axis=0, tiled=True),
        lax.all_gather(low1, "tensor", axis=0, tiled=True),
    )
    low1_all = low1_small
    qkv_arr = project_qkv(normed1_all, low1_all)
    qkv_seq = jnp.take(qkv_arr, order_row, axis=0)
    attended_seq, log_totals = attention_forward(qkv_seq, lengths_row, seq_len)
    attended = jnp.take(attended_seq.astype(jnp.bfloat16), inverse, axis=0)
    rows = attended
    mask_rows = group_mask
    part = matmul(rows, proj_joined)
    summed_attn = lax.psum_scatter(
        jnp.concatenate([part[:, :D], part[:, D:] * mask_rows], 1).astype(jnp.bfloat16),
        "tensor",
        scatter_dimension=0,
        tiled=True,
    ).astype(jnp.float32)
    proj_low = summed_attn[:, D:].astype(jnp.bfloat16)
    mid = inputs + summed_attn[:, :D] + matmul(proj_low, adapt_proj_out) + proj_bias
    normed2 = layer_norm(mid, norm2_gain, norm2_shift).astype(jnp.bfloat16)
    low2 = (matmul(normed2, adapt_up_in) * own_mask).astype(jnp.bfloat16)
    normed2_all, low2_small = (
        lax.all_gather(normed2, "tensor", axis=0, tiled=True),
        lax.all_gather(low2, "tensor", axis=0, tiled=True),
    )
    low2_all = low2_small
    upper = project_up(normed2_all, low2_all)
    active = gelu_tanh(upper).astype(jnp.bfloat16)
    rows = active
    mask_rows = group_mask
    part = matmul(rows, down_joined)
    summed_mlp = lax.psum_scatter(
        jnp.concatenate([part[:, :D], part[:, D:] * mask_rows], 1).astype(jnp.bfloat16),
        "tensor",
        scatter_dimension=0,
        tiled=True,
    ).astype(jnp.float32)
    down_low = summed_mlp[:, D:].astype(jnp.bfloat16)
    result = mid + summed_mlp[:, :D] + matmul(down_low, adapt_down_out) + down_bias
    grad_mlp = cotangent.astype(jnp.bfloat16)
    grad_down_low = (matmul_back(grad_mlp, adapt_down_out) * own_mask).astype(jnp.bfloat16)
    grad_down_out_part = matmul_over(down_low, grad_mlp)
    grad_mlp_all, grad_down_small = (
        lax.all_gather(grad_mlp, "tensor", axis=0, tiled=True),
        lax.all_gather(grad_down_low, "tensor", axis=0, tiled=True),
    )
    normed2_again, low2_again_small = (
        lax.all_gather(normed2, "tensor", axis=0, tiled=True),
        lax.all_gather(low2, "tensor", axis=0, tiled=True),
    )
    upper = project_up(normed2_again, low2_again_small)
    active = gelu_tanh(upper).astype(jnp.bfloat16)
    low2_all = low2_again_small
    grad_active = matmul_back(grad_mlp_all, down_weight) + matmul_back(
        grad_down_small, adapt_down_in
    )
    grad_down_in_part = matmul_over(active, grad_down_small)
    gelu_value, gelu_pull = jax.vjp(gelu_tanh, upper)
    grad_upper = gelu_pull(grad_active)[0].astype(jnp.bfloat16)
    grad_up_out_part = matmul_over(low2_all, grad_upper)
    rows = grad_upper
    part = matmul_back(rows, up_joined)
    summed_up = lax.psum_scatter(
        jnp.concatenate([part[:, :D], part[:, D:]], 1).astype(jnp.bfloat16),
        "tensor",
        scatter_dimension=0,
        tiled=True,
    ).astype(jnp.float32)
    grad_low2 = (summed_up[:, D:] * own_mask).astype(jnp.bfloat16)
    grad_up_in_part = matmul_over(normed2, grad_low2)
    grad_normed2 = summed_up[:, :D] + matmul_back(grad_low2, adapt_up_in)
    norm2_value, norm2_pull = jax.vjp(
        lambda values: layer_norm(values, norm2_gain, norm2_shift), mid
    )
    grad_mid = cotangent + norm2_pull(grad_normed2)[0]
    grad_attn = grad_mid.astype(jnp.bfloat16)
    grad_proj_low = (matmul_back(grad_attn, adapt_proj_out) * own_mask).astype(jnp.bfloat16)
    grad_proj_out_part = matmul_over(proj_low, grad_attn)
    grad_attn_all, grad_proj_small = (
        lax.all_gather(grad_attn, "tensor", axis=0, tiled=True),
        lax.all_gather(grad_proj_low, "tensor", axis=0, tiled=True),
    )
    grad_attended = matmul_back(grad_attn_all, proj_weight) + matmul_back(
        grad_proj_small, adapt_proj_in
    )
    grad_proj_in_part = matmul_over(attended, grad_proj_small)
    grad_attended_seq = jnp.take(grad_attended, order_row, axis=0).astype(jnp.bfloat16)
    normed1_again, low1_again_small = (
        lax.all_gather(normed1, "tensor", axis=0, tiled=True),
        lax.all_gather(low1, "tensor", axis=0, tiled=True),
    )
    qkv_seq = jnp.take(project_qkv(normed1_again, low1_again_small), order_row, axis=0)
    low1_all = low1_again_small
    grad_qkv_seq = attention_backward(qkv_seq, grad_attended_seq, log_totals, lengths_row, seq_len)
    grad_qkv = jnp.take(grad_qkv_seq.astype(jnp.bfloat16), inverse, axis=0)
    grad_qkv_out_part = jnp.einsum(
        "ra,rkc->akc", low1_all, grad_qkv, preferred_element_type=jnp.float32
    )
    rows = grad_qkv
    part = jnp.einsum("rkc,dkc->rd", rows, qkv_joined, preferred_element_type=jnp.float32)
    summed_qkv = lax.psum_scatter(
        jnp.concatenate([part[:, :D], part[:, D:]], 1).astype(jnp.bfloat16),
        "tensor",
        scatter_dimension=0,
        tiled=True,
    ).astype(jnp.float32)
    grad_low1 = (summed_qkv[:, D:] * own_mask).astype(jnp.bfloat16)
    grad_qkv_in_part = matmul_over(normed1, grad_low1)
    grad_normed1 = summed_qkv[:, :D] + matmul_back(grad_low1, adapt_qkv_in)
    norm1_value, norm1_pull = jax.vjp(
        lambda values: layer_norm(values, norm1_gain, norm1_shift), inputs
    )
    grad_input = grad_mid + norm1_pull(grad_normed1)[0]
    wide = lax.psum(
        (grad_qkv_in_part, grad_proj_out_part, grad_up_in_part, grad_down_out_part),
        ("dp", "tensor"),
    )
    narrow = (
        lax.psum(grad_qkv_out_part.astype(jnp.bfloat16), "dp").astype(jnp.float32),
        lax.psum(grad_proj_in_part.astype(jnp.bfloat16), "dp").astype(jnp.float32),
        lax.psum(grad_up_out_part.astype(jnp.bfloat16), "dp").astype(jnp.float32),
        lax.psum(grad_down_in_part.astype(jnp.bfloat16), "dp").astype(jnp.float32),
    )
    return (
        result,
        grad_input,
        wide[0],
        narrow[0],
        narrow[1],
        wide[1],
        wide[2],
        narrow[2],
        narrow[3],
        wide[3],
    )


def solution(mesh):
    in_specs = (
        P(("dp", "tensor"), None),
        P(("dp", "tensor"), None),
        P("dp", None),
        P("dp", None),
        P("dp", None),
        P(),
        P(),
        P(None, None, "tensor"),
        P(None, "tensor"),
        P("tensor", None),
        P(),
        P(),
        P(),
        P(None, "tensor"),
        P("tensor"),
        P("tensor", None),
        P(),
        P(),
        P(None, None, "tensor"),
        P("tensor", None),
        P(),
        P(),
        P(None, "tensor"),
        P("tensor", None),
        P(),
    )
    out_specs = (
        P(("dp", "tensor"), None),
        P(("dp", "tensor"), None),
        P(),
        P(None, None, "tensor"),
        P("tensor", None),
        P(),
        P(),
        P(None, "tensor"),
        P("tensor", None),
        P(),
    )
    return jax.shard_map(body, mesh=mesh, in_specs=in_specs, out_specs=out_specs, check_vma=False)
```

profile of v0, /device:TPU:0, one launch (start us, length us, event | category | flops | bytes accessed | tf_op | source)
XLA Modules:
  0.0 638.7 jit_solution(10005724395536461428)
XLA Ops:
  20.2 8.9 %all_gather.29 = bf16[1024,128]{1,0:T(8,128)(2,1)S(1)} all-gather(bf16[256,128]{1,0:T(8,128)(2,1)S(1)} %fusion.97), channel_id=1, replica_groups=mesh['dp'=8,'tensor'=4] {'tensor'}, dimensions={0}, use_global_device_ids=true | all-gather | bytes 327680 | tf_op jit(solution)/shard_map/all_gather | solution.py:197
  31.9 6.9 %all-gather.5.cloned.1.call-done = bf16[1024,1024]{1,0:T(8,128)(2,1)} async-done(((bf16[256,1024]{1,0:T(8,128)(2,1)}), bf16[1024,1024]{1,0:T(8,128)(2,1)}) %all-gather.5.cloned.1.call-update) | async-done | bytes 2097168 | tf_op jit(solution)/shard_map/all_gather | solution.py:196
  46.0 10.1 %gather_fusion.2 = bf16[1024,3,256]{2,1,0:T(4,128)(2,1)} fusion(bf16[1024,3,256]{2,1,0:T(4,128)(2,1)} %copy.65, s32[1024]{0:T(1024)S(1)} %fusion.129), kind=kCustom, calls=%fused_computation.clone | custom fusion | bytes 3149824 | tf_op jit(solution)/shard_map/jit(_take)/gather | solution.py:201
  56.1 6.3 broadcast_select_fusion.1
  65.3 15.9 %while.32 = (s32[]{:T(128)}, bf16[2,512,256]{1,2,0:T(8,128)(2,1)S(1)}, f32[2,4,512]{2,1,0:T(4,128)S(1)}, bf16[1024,3,4,64]{0,3,2,1:T(8,128)(2,1)S(1)}, s32[2]{0:...) while((s32[]{:T(128)}, ...), condition=%wide.region_7.9_spmd, body=%wide.region_4.8_spmd.sunk | while | flops 281541120 | bytes 18417900 | solution.py:72
  81.4 4.4 gather_fusion
  91.6 32.2 %reduce-scatter.5.cloned.1.call-done = bf16[256,1152]{1,0:T(8,128)(2,1)} async-done(((bf16[1024,1152]{1,0:T(8,128)(2,1)}), bf16[256,1152]{1,0:T(8,128)(2,1)}) %reduce-scatter.5.cloned.1.call-update) | async-done | bytes 589840 | tf_op jit(solution)/shard_map/reduce_scatter | solution.py:207
  129.0 6.4 %all_gather.33 = bf16[1024,128]{1,0:T(8,128)(2,1)} all-gather(bf16[256,128]{1,0:T(8,128)(2,1)S(1)} %fusion.99), channel_id=1, replica_groups=mesh['dp'=8,'tensor'=4] {'tensor'}, dimensions={0}, use_global_device_ids=true | all-gather | bytes 327680 | tf_op jit(solution)/shard_map/all_gather | solution.py:240
  135.4 13.3 %all-gather.9.cloned.1.call-done = bf16[1024,1024]{1,0:T(8,128)(2,1)} async-done(((bf16[256,1024]{1,0:T(8,128)(2,1)}), bf16[1024,1024]{1,0:T(8,128)(2,1)}) %all-gather.9.cloned.1.call-update) | async-done | bytes 2097168 | tf_op jit(solution)/shard_map/all_gather | solution.py:239
  148.7 6.6 %fusion.153 = f32[1024,1024]{1,0:T(8,128)} fusion(bf16[1024,1024]{1,0:T(8,128)(2,1)} %all-gather.9.cloned.1.call-done, bf16[1024,1024]{1,0:T(8,128)(2,1)} %param.46), kind=kOutput, calls=%fused_computation.219 | convolution fusion | flops 2147483648 | bytes 8388608 | tf_op jit(solution)/shard_map/dot_general | solution.py:25
  155.6 5.8 all_gather.31
  161.4 12.0 %all-gather.7.cloned.1.call-done = bf16[1024,1024]{1,0:T(8,128)(2,1)} async-done(((bf16[256,1024]{1,0:T(8,128)(2,1)}), bf16[1024,1024]{1,0:T(8,128)(2,1)}) %all-gather.7.cloned.1.call-update) | async-done | bytes 2097168 | tf_op jit(solution)/shard_map/all_gather | solution.py:218
  173.4 4.6 fusion.152
  190.7 33.2 %reduce-scatter.9.cloned.1.call-done = bf16[256,1152]{1,0:T(8,128)(2,1)} async-done(((bf16[1024,1152]{1,0:T(8,128)(2,1)}), bf16[256,1152]{1,0:T(8,128)(2,1)}) %reduce-scatter.9.cloned.1.call-update) | async-done | bytes 589840 | tf_op jit(solution)/shard_map/reduce_scatter | solution.py:258
  229.6 6.5 %fusion.77 = bf16[1024,1152]{1,0:T(8,128)(2,1)S(1)} fusion(bf16[1024,128]{1,0:T(8,128)(2,1)S(1)} %copy-done.64, bf16[1024,1024]{1,0:T(8,128)(2,1)} %param.46, f32[1024,1024]{1,0:T(8,128)} %copy-done.18), kind=kOutput, calls=%fused_computation.87 | convolution fusion | flops 2430074880 | bytes 8912896 | tf_op jit(solution)/shard_map/dot_general | solution.py:21
  240.9 4.8 convolution_convert_fusion.1
  246.1 6.3 all_gather.35
  257.4 5.5 gather_fusion.1
  266.1 62.1 %while.33 = (s32[]{:T(128)}, bf16[2,512,4,64]{1,3,2,0:T(8,128)(2,1)}, bf16[2,512,4,64]{1,3,2,0:T(8,128)(2,1)}, bf16[2,512,4,64]{1,3,2,0:T(8,128)(2,1)}, bf16[102...) while((s32[]{:T(128)}, ...), condition=%wide.region_17.19_spmd, body=%wide.region_15.18_spmd.sunk | while | flops 686298624 | bytes 57437636 | solution.py:112
  277.6 7.9 %fusion.232 = bf16[2,512,4,64]{1,3,2,0:T(8,128)(2,1)} fusion(bf16[2,512,4,64]{1,3,2,0:T(8,128)(2,1)} %get-tuple-element.493, s32[]{:T(128)S(6)} %copy.112, f32[4,512,512]{1,2,0:T(8,128)} %subtract_exponential_fusion.3, f32[4,512,512]{1,2,0:T(8,128)} %fusion.230, bf16[1024,1,4,64]{0,3,2,1:T(8,128)(2,1)} %copy-done.5, s32[]{:T(128)S(6)} %select_n.203), kind=kOutput, calls=%fused_computation.43.clone.1 | convolution fusion | flops 139463168 | bytes 17563656 | tf_op jit(solution)/shard_map/while/body/eval_jaxpr/hqk,qhc->khc/dot_general | solution.py:102
  285.6 8.0 %fusion.231 = bf16[2,512,4,64]{1,3,2,0:T(8,128)(2,1)} fusion(bf16[2,512,4,64]{1,3,2,0:T(8,128)(2,1)} %get-tuple-element.492, s32[]{:T(128)S(6)} %copy.112, f32[4,512,512]{1,2,0:T(8,128)} %subtract_exponential_fusion.3, f32[4,512,512]{1,2,0:T(8,128)} %fusion.230, bf16[1024,1,4,64]{0,3,2,1:T(8,128)(2,1)} %copy-done.4, s32[]{:T(128)S(6)} %select_n.203), kind=kOutput, calls=%fused_computation.41.clone.1 | convolution fusion | flops 139463168 | bytes 17563656 | tf_op jit(solution)/shard_map/while/body/eval_jaxpr/hqk,khc->qhc/dot_general | solution.py:101
  308.7 7.9 %fusion.232 = bf16[2,512,4,64]{1,3,2,0:T(8,128)(2,1)} fusion(bf16[2,512,4,64]{1,3,2,0:T(8,128)(2,1)} %get-tuple-element.493, s32[]{:T(128)S(6)} %copy.112, f32[4,512,512]{1,2,0:T(8,128)} %subtract_exponential_fusion.3, f32[4,512,512]{1,2,0:T(8,128)} %fusion.230, bf16[1024,1,4,64]{0,3,2,1:T(8,128)(2,1)} %copy-done.5, s32[]{:T(128)S(6)} %select_n.203), kind=kOutput, calls=%fused_computation.43.clone.1 | convolution fusion | flops 139463168 | bytes 17563656 | tf_op jit(solution)/shard_map/while/body/eval_jaxpr/hqk,qhc->khc/dot_general | solution.py:102
  316.6 8.0 %fusion.231 = bf16[2,512,4,64]{1,3,2,0:T(8,128)(2,1)} fusion(bf16[2,512,4,64]{1,3,2,0:T(8,128)(2,1)} %get-tuple-element.492, s32[]{:T(128)S(6)} %copy.112, f32[4,512,512]{1,2,0:T(8,128)} %subtract_exponential_fusion.3, f32[4,512,512]{1,2,0:T(8,128)} %fusion.230, bf16[1024,1,4,64]{0,3,2,1:T(8,128)(2,1)} %copy-done.4, s32[]{:T(128)S(6)} %select_n.203), kind=kOutput, calls=%fused_computation.41.clone.1 | convolution fusion | flops 139463168 | bytes 17563656 | tf_op jit(solution)/shard_map/while/body/eval_jaxpr/hqk,khc->qhc/dot_general | solution.py:101
  336.9 4.8 reshape.386
  343.0 4.8 reshape.387
  347.8 5.8 pad_maximum_fusion.2
  353.6 10.2 %gather_fusion.3 = bf16[1024,3,256]{2,1,0:T(4,128)(2,1)} fusion(bf16[1024,3,256]{2,1,0:T(4,128)(2,1)} %pad_maximum_fusion.2, s32[1024]{0:T(1024)S(1)} %copy-done.40), kind=kCustom, calls=%fused_computation.1.clone | custom fusion | bytes 3149824 | tf_op jit(solution)/shard_map/jit(_take)/gather | solution.py:290
  363.8 5.3 broadcast_select_fusion
  371.9 5.7 bitcast_convert_fusion
  386.0 61.0 %all-reduce.7.cloned.1.call-done = (bf16[128,3,256]{2,0,1:T(8,128)(2,1)}, bf16[256,128]{1,0:T(8,128)(2,1)}, bf16[128,1024]{1,0:T(8,128)(2,1)}, bf16[1024,128]{1,0:T(8,128)(2,1)}) async-done(((bf16[128,3,256]{2,0,1:T(8,128)(2,1)}, bf16[256,128]{1,0:T(8,128)(2,1)}, bf16[128,1024]{1,0:T(8,128)(2,1)}, bf16[1024,128]{1,0:T(8,128)(2,1)}), (bf16[128,3,256]{2,0,1:T(8,128)(2,1)}, bf16[256,128]{1,0:T(8,128)(2,1)}, ...) | async-done | bytes 786448 | tf_op jit(solution)/shard_map/psum | solution.py:314
  453.7 27.9 %reduce-scatter.11.cloned.1.call-done = bf16[256,1152]{1,0:T(8,128)(2,1)} async-done(((bf16[1024,1152]{1,0:T(8,128)(2,1)}), bf16[256,1152]{1,0:T(8,128)(2,1)}) %reduce-scatter.11.cloned.1.call-update) | async-done | bytes 589840 | tf_op jit(solution)/shard_map/reduce_scatter | solution.py:296
  489.3 134.8 %all-reduce.5.cloned.1.call-done = (f32[1024,128]{1,0:T(8,128)}, f32[128,1024]{1,0:T(8,128)}, f32[1024,128]{1,0:T(8,128)}, f32[128,1024]{1,0:T(8,128)}) async-done(((f32[1024,128]{1,0:T(8,128)}, f32[128,1024]{1,0:T(8,128)}, f32[1024,128]{1,0:T(8,128)}, f32[128,1024]{1,0:T(8,128)}), (f32[1024,128]{1,0:T(8,128)}, f32[128,1024]{1,0:T(8,128)}, f32[1024,128]{1,0:T(8,128)}, ...) | async-done | bytes 2097168 | tf_op jit(solution)/shard_map/psum | solution.py:309
  (293 shorter events, 147.0 us)
Async XLA Ops:
  7.2 148.1 %copy-start = (bf16[1024,128]{1,0:T(8,128)(2,1)S(1)}, bf16[1024,128]{1,0:T(8,128)(2,1)}, u32[]{:S(2)}) copy-start(bf16[1024,128]{1,0:T(8,128)(2,1)} %param.52) | copy-start | bytes 786436
  7.2 31.6 %all-gather.5.cloned.1.call-start = ((), (), s32[]{:S(2)}) async-start(), calls=%async_computation.4 | async-start | bytes 2621440 | tf_op jit(solution)/shard_map/all_gather | solution.py:196
  8.5 30.4 %copy-start.38 = (f32[256]{0:T(256)}, f32[256]{0:T(256)S(1)}, u32[]{:S(2)}) copy-start(f32[256]{0:T(256)S(1)} %broadcast_multiply_fusion.1) | copy-start | bytes 3076
  9.8 29.0 %copy-start.55 = (f32[256]{0:T(256)}, f32[256]{0:T(256)S(1)}, u32[]{:S(2)}) copy-start(f32[256]{0:T(256)S(1)} %fusion.103) | copy-start | bytes 3076
  9.8 29.0 %copy-start.46 = (f32[256]{0:T(256)}, f32[256]{0:T(256)S(1)}, u32[]{:S(2)}) copy-start(f32[256]{0:T(256)S(1)} %fusion.138) | copy-start | bytes 3076
  12.0 111.8 %reduce-scatter.5.cloned.1.call-start = ((), (), s32[]{:S(2)}) async-start(), calls=%async_computation.5 | async-start | bytes 2949120 | tf_op jit(solution)/shard_map/reduce_scatter | solution.py:207
  18.5 24.1 %copy-start.36 = (s32[1024]{0:T(1024)}, s32[1024]{0:T(1024)S(1)}, u32[]{:S(2)}) copy-start(s32[1024]{0:T(1024)S(1)} %fusion.125) | copy-start | bytes 12292
  31.2 24.9 %copy-start.49 = (pred[1024]{0:T(1024)(128)(4,1)}, pred[1024]{0:T(1024)(128)(4,1)S(1)}, u32[]{:S(2)}) copy-start(pred[1024]{0:T(1024)(128)(4,1)S(1)} %compare_and_fusion) | copy-start | bytes 3076
  88.9 34.9 %copy-start.2 = (bf16[256,1024]{1,0:T(8,128)(2,1)S(1)}, bf16[256,1024]{1,0:T(8,128)(2,1)}, u32[]{:S(2)}) copy-start(bf16[256,1024]{1,0:T(8,128)(2,1)} %param.31) | copy-start | bytes 1572868
  90.6 58.1 %all-gather.9.cloned.1.call-start = ((), (), s32[]{:S(2)}) async-start(), calls=%async_computation.8 | async-start | bytes 2621440 | tf_op jit(solution)/shard_map/all_gather | solution.py:239
  91.6 81.8 %all-gather.7.cloned.1.call-start = ((), (), s32[]{:S(2)}) async-start(), calls=%async_computation.6 | async-start | bytes 2621440 | tf_op jit(solution)/shard_map/all_gather | solution.py:218
  127.5 96.4 %reduce-scatter.9.cloned.1.call-start = ((), (), s32[]{:S(2)}) async-start(), calls=%async_computation.9 | async-start | bytes 2949120 | tf_op jit(solution)/shard_map/reduce_scatter | solution.py:258
  135.4 19.9 %copy-start.15 = (bf16[256,1024]{1,0:T(8,128)(2,1)S(1)}, bf16[256,1024]{1,0:T(8,128)(2,1)}, u32[]{:S(2)}) copy-start(bf16[256,1024]{1,0:T(8,128)(2,1)} %add_convert_fusion.1) | copy-start | bytes 1572868
  190.7 35.7 %copy-start.57 = (f32[256]{0:T(256)S(1)}, f32[256]{0:T(256)}, u32[]{:S(2)}) copy-start(f32[256]{0:T(256)} %copy-done.56) | copy-start | bytes 3076
  190.7 35.8 %copy-start.42 = (f32[256]{0:T(256)S(1)}, f32[256]{0:T(256)}, u32[]{:S(2)}) copy-start(f32[256]{0:T(256)} %copy-done.41) | copy-start | bytes 3076
  190.7 35.8 %copy-start.54 = (f32[256]{0:T(256)S(1)}, f32[256]{0:T(256)}, u32[]{:S(2)}) copy-start(f32[256]{0:T(256)} %copy-done.53) | copy-start | bytes 3076
  190.7 63.9 %all-gather.11.cloned.1.call-start = ((), (), s32[]{:S(2)}) async-start(), calls=%async_computation.10 | async-start | bytes 2621440 | tf_op jit(solution)/shard_map/all_gather | solution.py:275
  228.9 150.7 %reduce-scatter.7.cloned.1.call-start = ((), (), s32[]{:S(2)}) async-start(), calls=%async_computation.7 | async-start | bytes 2949120 | tf_op jit(solution)/shard_map/reduce_scatter | solution.py:227
  245.7 201.2 %all-reduce.7.cloned.1.call-start = ((), (), s32[]{:S(2)}) async-start(), calls=%async_computation.13 | async-start | bytes 1572864 | tf_op jit(solution)/shard_map/psum | solution.py:314
  353.6 16.8 %copy-start.20 = (bf16[1024,128]{1,0:T(8,128)(2,1)S(1)}, bf16[1024,128]{1,0:T(8,128)(2,1)}, u32[]{:S(2)}) copy-start(bf16[1024,128]{1,0:T(8,128)(2,1)} %copy-done.19) | copy-start | bytes 786436
  371.6 110.1 %reduce-scatter.11.cloned.1.call-start = ((), (), s32[]{:S(2)}) async-start(), calls=%async_computation.11 | async-start | bytes 2949120 | tf_op jit(solution)/shard_map/reduce_scatter | solution.py:296
  377.6 246.5 %all-reduce.5.cloned.1.call-start = ((), (), s32[]{:S(2)}) async-start(), calls=%async_computation.12 | async-start | bytes 4194304 | tf_op jit(solution)/shard_map/psum | solution.py:309
  379.6 104.2 %copy-start.14 = (bf16[256,1024]{1,0:T(8,128)(2,1)S(1)}, bf16[256,1024]{1,0:T(8,128)(2,1)}, u32[]{:S(2)}) copy-start(bf16[256,1024]{1,0:T(8,128)(2,1)} %fusion.106) | copy-start | bytes 1572868
  386.0 99.1 %copy-start.3 = (bf16[256,1024]{1,0:T(8,128)(2,1)S(1)}, bf16[256,1024]{1,0:T(8,128)(2,1)}, u32[]{:S(2)}) copy-start(bf16[256,1024]{1,0:T(8,128)(2,1)} %param.31) | copy-start | bytes 1572868
  386.0 99.1 %copy-start.28 = (bf16[1024,128]{1,0:T(8,128)(2,1)S(1)}, bf16[1024,128]{1,0:T(8,128)(2,1)}, u32[]{:S(2)}) copy-start(bf16[1024,128]{1,0:T(8,128)(2,1)} %param.48) | copy-start | bytes 786436
  386.0 99.1 %copy-start.39 = (f32[256]{0:T(256)S(1)}, f32[256]{0:T(256)}, u32[]{:S(2)}) copy-start(f32[256]{0:T(256)} %copy-done.38) | copy-start | bytes 3076
  386.0 99.1 %copy-start.43 = (f32[1024]{0:T(1024)S(1)}, f32[1024]{0:T(1024)}, u32[]{:S(2)}) copy-start(f32[1024]{0:T(1024)} %param.36) | copy-start | bytes 12292
  450.2 37.3 %copy-start.47 = (f32[256]{0:T(256)S(1)}, f32[256]{0:T(256)}, u32[]{:S(2)}) copy-start(f32[256]{0:T(256)} %copy-done.46) | copy-start | bytes 3076
  453.7 34.1 %copy-start.8 = (f32[256,1024]{1,0:T(8,128)S(1)}, f32[256,1024]{1,0:T(8,128)}, u32[]{:S(2)}) copy-start(f32[256,1024]{1,0:T(8,128)} %param.32) | copy-start | bytes 3145732
  453.7 34.1 %copy-start.10 = (f32[256,1024]{1,0:T(8,128)S(1)}, f32[256,1024]{1,0:T(8,128)}, u32[]{:S(2)}) copy-start(f32[256,1024]{1,0:T(8,128)} %copy-done.9) | copy-start | bytes 3145732
  453.7 34.1 %copy-start.52 = (f32[256]{0:T(256)S(1)}, f32[256]{0:T(256)}, u32[]{:S(2)}) copy-start(f32[256]{0:T(256)} %copy-done.51) | copy-start | bytes 3076
  487.8 143.8 %copy-start.1 = (bf16[1024,128]{1,0:T(8,128)(2,1)S(1)}, bf16[1024,128]{1,0:T(8,128)(2,1)}, u32[]{:S(2)}) copy-start(bf16[1024,128]{1,0:T(8,128)(2,1)} %param.52) | copy-start | bytes 786436
  (51 other events, 271.6 us)
Sparse Core Ops, SparseCore 0:
  12.1 26.6 all-gather.4
  90.7 33.0 reduce-scatter.4
  126.0 22.5 all-gather.8
  150.7 22.5 all-gather.6
  190.8 33.0 reduce-scatter.8
  229.0 23.5 all-gather.10
  255.1 33.1 reduce-scatter.6
  371.7 75.2 all-reduce.6
  449.5 32.0 reduce-scatter.10
  489.2 134.8 all-reduce.4
where the time goes:
time: 643 us; the launch traced here: 639 us
  waiting for transfers between devices  321 us (50%)
  matrix products  123 us (19%)
  local copies, waits for them, and re-layouts  87.2 us (14%)
  other arithmetic  53.3 us (8%)
  blocking collectives  27.4 us (4%)
  between operations  15.3 us (2%)
  loops' own time  10.6 us (2%)
    psum x1, waiting for transfers between devices, body(): lax.psum((grad_qkv_in_part, grad_proj_out_part, grad_up_in_part, grad_dow...  135 us
    reduce_scatter x2, waiting for transfers between devices, body(): lax.psum_scatter(jnp.concatenate([part[:, :D], part[:, D:]], 1).astype(jn...  61 us
    psum x1, waiting for transfers between devices, body(): lax.psum(grad_qkv_out_part.astype(jnp.bfloat16), 'dp').astype(jnp.float32)  61 us
    reduce_scatter x2, waiting for transfers between devices, body(): lax.psum_scatter(jnp.concatenate([part[:, :D], part[:, D:] * mask_rows],...  32.2 us
    dot_general x9, matrix products, matmul_back(): lax.dot_general(left, right, (((1,), (1,)), ((), ())), preferred_element_...  21.5 us
    another operation x6, local copies, waits for them, and re-layouts, attention_backward(): return jnp.stack([grad_query, grad_key, grad_value], 1)  19.6 us
    dot_general x8, matrix products, matmul(): return jnp.dot(left, right, preferred_element_type=jnp.float32)  19.2 us
    unnamed x134, local copies, waits for them, and re-layouts  17.1 us
  transfers between devices with their start and end apart: 10, of which 8 were waited for; matrix products, arithmetic and copies ran while one was open for 28% of the time, Pallas kernels for 0%

commit v1 on v0

--- a/solution.py
+++ b/solution.py
@@ -9,6 +9,27 @@
 RANK = 16
 EPSILON = 1e-05
 NEGATIVE = -1000000000.0
+
+
+def ring_gather(x, axis, dim):
+    length, index, rows = (lax.axis_size(axis), lax.axis_index(axis), x.shape[dim])
+    right = [(i, (i + 1) % length) for i in range(length)]
+    left = [(i, (i - 1) % length) for i in range(length)]
+    result = jnp.zeros((*x.shape[:dim], length * rows, *x.shape[dim + 1 :]), x.dtype)
+    result = lax.dynamic_update_slice_in_dim(result, x, index * rows, axis=dim)
+    from_left = from_right = x
+    halfway = length // 2
+    for turn in range(1, halfway + 1):
+        from_left = lax.ppermute(from_left, axis, right)
+        result = lax.dynamic_update_slice_in_dim(
+            result, from_left, (index - turn) % length * rows, axis=dim
+        )
+        if turn < length - halfway:
+            from_right = lax.ppermute(from_right, axis, left)
+            result = lax.dynamic_update_slice_in_dim(
+                result, from_right, (index + turn) % length * rows, axis=dim
+            )
+    return result
 
 
 def layer_norm(values, gain, shift):
@@ -236,7 +257,7 @@
     grad_down_low = (matmul_back(grad_mlp, adapt_down_out) * own_mask).astype(jnp.bfloat16)
     grad_down_out_part = matmul_over(down_low, grad_mlp)
     grad_mlp_all, grad_down_small = (
-        lax.all_gather(grad_mlp, "tensor", axis=0, tiled=True),
+        ring_gather(grad_mlp, "tensor", 0),
         lax.all_gather(grad_down_low, "tensor", axis=0, tiled=True),
     )
     normed2_again, low2_again_small = (

time: 643 us -> 646 us (level)
  waiting for transfers between devices: 321 us -> 301 us
  blocking collectives: 27.4 us -> 45.1 us
    all_gather x1, blocking collectives: 6.41 us -> 24 us  [body(): lax.all_gather(grad_down_low, 'tensor', axis=0, tiled=True)]
    all_gather x1 -> x0, waiting for transfers between devices: 13.3 us -> none  [body(): lax.all_gather(grad_mlp, 'tensor', axis=0, tiled=True)]
    all_gather x1, waiting for transfers between devices: 12 us -> 0.01 us  [body(): lax.all_gather(normed2, 'tensor', axis=0, tiled=True)]
    unnamed x134 -> x150, local copies, waits for them, and re-layouts: 17.1 us -> 16.1 us
  transfers between devices with their start and end apart: 10 -> 12, of which waited for: 8 -> 7; matrix products, arithmetic and copies ran while one was open for 28% -> 27% of each run, Pallas kernels for 0% -> 0%
where the time goes in v1:
time: 646 us; the launch traced here: 642 us
  waiting for transfers between devices  301 us (47%)
  matrix products  124 us (19%)
  local copies, waits for them, and re-layouts  90.6 us (14%)
  other arithmetic  52.5 us (8%)
  blocking collectives  45.1 us (7%)
  between operations  15.1 us (2%)
  loops' own time  10.6 us (2%)
    psum x1, waiting for transfers between devices, body(): lax.psum((grad_qkv_in_part, grad_proj_out_part, grad_up_in_part, grad_dow...  135 us
    reduce_scatter x2, waiting for transfers between devices, body(): lax.psum_scatter(jnp.concatenate([part[:, :D], part[:, D:]], 1).astype(jn...  61.8 us
    psum x1, waiting for transfers between devices, body(): lax.psum(grad_qkv_out_part.astype(jnp.bfloat16), 'dp').astype(jnp.float32)  60.9 us
    reduce_scatter x2, waiting for transfers between devices, body(): lax.psum_scatter(jnp.concatenate([part[:, :D], part[:, D:] * mask_rows],...  33.2 us
    all_gather x1, blocking collectives, body(): lax.all_gather(grad_down_low, 'tensor', axis=0, tiled=True)  24 us
    dot_general x9, matrix products, matmul_back(): lax.dot_general(left, right, (((1,), (1,)), ((), ())), preferred_element_...  22.7 us
    dot_general x8, matrix products, matmul(): return jnp.dot(left, right, preferred_element_type=jnp.float32)  19.3 us
    another operation x6, local copies, waits for them, and re-layouts, attention_backward(): return jnp.stack([grad_query, grad_key, grad_value], 1)  18.7 us
  transfers between devices with their start and end apart: 12, of which 7 were waited for; matrix products, arithmetic and copies ran while one was open for 27% of the time, Pallas kernels for 0%

profile of v1, /device:TPU:0, one launch (start us, length us, event | category | flops | bytes accessed | tf_op | source)
XLA Modules:
  0.0 641.6 jit_solution(13292792012993617924)
XLA Ops:
  13.0 4.3 scatter_custom_fusion
  20.6 9.1 %all_gather.26 = bf16[1024,128]{1,0:T(8,128)(2,1)S(1)} all-gather(bf16[256,128]{1,0:T(8,128)(2,1)S(1)} %fusion.97), channel_id=1, replica_groups=mesh['dp'=8,'tensor'=4] {'tensor'}, dimensions={0}, use_global_device_ids=true | all-gather | bytes 327680 | tf_op jit(solution)/shard_map/all_gather | solution.py:218
  30.5 8.5 %all-gather.4.cloned.1.call-done = bf16[1024,1024]{1,0:T(8,128)(2,1)} async-done(((bf16[256,1024]{1,0:T(8,128)(2,1)}), bf16[1024,1024]{1,0:T(8,128)(2,1)}) %all-gather.4.cloned.1.call-update) | async-done | bytes 2097168 | tf_op jit(solution)/shard_map/all_gather | solution.py:217
  44.3 8.7 %gather_fusion.2 = bf16[1024,3,256]{2,1,0:T(4,128)(2,1)} fusion(bf16[1024,3,256]{2,1,0:T(4,128)(2,1)S(1)} %copy.65, s32[1024]{0:T(1024)S(1)} %fusion.129), kind=kCustom, calls=%fused_computation.clone | custom fusion | bytes 3149824 | tf_op jit(solution)/shard_map/jit(_take)/gather | solution.py:222
  53.0 6.3 broadcast_select_fusion.1
  62.2 17.3 %while.32 = (s32[]{:T(128)}, bf16[2,512,256]{1,2,0:T(8,128)(2,1)}, f32[2,4,512]{2,1,0:T(4,128)S(1)}, bf16[1024,3,4,64]{0,3,2,1:T(8,128)(2,1)S(1)}, s32[2]{0:T(12...) while((s32[]{:T(128)}, bf16[2,512,256]{1,2,0:T(8,128)(2,1)}, ...), condition=%wide.region_7.9_spmd, body=%wide.region_4.8_spmd.sunk | while | flops 281541120 | bytes 18417900 | solution.py:93
  80.8 4.4 gather_fusion
  89.4 33.2 %reduce-scatter.5.cloned.1.call-done = bf16[256,1152]{1,0:T(8,128)(2,1)} async-done(((bf16[1024,1152]{1,0:T(8,128)(2,1)}), bf16[256,1152]{1,0:T(8,128)(2,1)}) %reduce-scatter.5.cloned.1.call-update) | async-done | bytes 589840 | tf_op jit(solution)/shard_map/reduce_scatter | solution.py:228
  133.5 24.0 %all_gather.29 = bf16[1024,128]{1,0:T(8,128)(2,1)S(1)} all-gather(bf16[256,128]{1,0:T(8,128)(2,1)S(1)} %fusion.99), channel_id=1, replica_groups=mesh['dp'=8,'tensor'=4] {'tensor'}, dimensions={0}, use_global_device_ids=true | all-gather | bytes 327680 | tf_op jit(solution)/shard_map/all_gather | solution.py:261
  167.5 5.8 all_gather.28
  173.3 4.6 fusion.152
  180.8 8.1 %fusion.76 = bf16[1024,1024]{1,0:T(8,128)(2,1)S(1)} fusion(f32[1024,1024]{1,0:T(8,128)S(1)} %add_add_fusion, f32[1024,1024]{1,0:T(8,128)S(1)} %copy-done.16, bf16[1024,1024]{1,0:T(8,128)(2,1)} %constant_dynamic-update-slice_fusion.1, bf16[1024,1024]{1,0:T(8,128)(2,1)S(1)} %copy-done.72), kind=kOutput, calls=%fused_computation.79 | convolution fusion | flops 2169503744 | bytes 14680064 | tf_op jit(solution)/shard_map/dot_general | solution.py:46
  190.3 4.2 convolution_convert_fusion
  194.6 34.0 %reduce-scatter.9.cloned.1.call-done = bf16[256,1152]{1,0:T(8,128)(2,1)} async-done(((bf16[1024,1152]{1,0:T(8,128)(2,1)}), bf16[256,1152]{1,0:T(8,128)(2,1)}) %reduce-scatter.9.cloned.1.call-update) | async-done | bytes 589840 | tf_op jit(solution)/shard_map/reduce_scatter | solution.py:279
  233.9 6.5 %fusion.77 = bf16[1024,1152]{1,0:T(8,128)(2,1)S(1)} fusion(bf16[1024,128]{1,0:T(8,128)(2,1)S(1)} %copy-done.35, bf16[1024,1024]{1,0:T(8,128)(2,1)} %param.46, f32[1024,1024]{1,0:T(8,128)} %copy-done.17), kind=kOutput, calls=%fused_computation.87 | convolution fusion | flops 2430074880 | bytes 8912896 | tf_op jit(solution)/shard_map/dot_general | solution.py:42
  245.2 4.8 convolution_convert_fusion.1
  250.4 6.3 all_gather.31
  261.7 5.5 gather_fusion.1
  270.5 62.6 %while.33 = (s32[]{:T(128)}, bf16[2,512,4,64]{1,3,2,0:T(8,128)(2,1)}, bf16[2,512,4,64]{1,3,2,0:T(8,128)(2,1)}, bf16[2,512,4,64]{1,3,2,0:T(8,128)(2,1)}, bf16[102...) while((s32[]{:T(128)}, ...), condition=%wide.region_17.19_spmd, body=%wide.region_15.18_spmd.sunk | while | flops 686298624 | bytes 57437636 | solution.py:133
  282.0 8.0 %fusion.232 = bf16[2,512,4,64]{1,3,2,0:T(8,128)(2,1)} fusion(bf16[2,512,4,64]{1,3,2,0:T(8,128)(2,1)} %get-tuple-element.495, s32[]{:T(128)S(6)} %copy.116, f32[4,512,512]{1,2,0:T(8,128)} %subtract_exponential_fusion.3, f32[4,512,512]{1,2,0:T(8,128)} %fusion.230, bf16[1024,1,4,64]{0,3,2,1:T(8,128)(2,1)} %copy-done.5, s32[]{:T(128)S(6)} %select_n.231), kind=kOutput, calls=%fused_computation.43.clone.1 | convolution fusion | flops 139463168 | bytes 17563656 | tf_op jit(solution)/shard_map/while/body/eval_jaxpr/hqk,qhc->khc/dot_general | solution.py:123
  290.0 8.2 %fusion.231 = bf16[2,512,4,64]{1,3,2,0:T(8,128)(2,1)} fusion(bf16[2,512,4,64]{1,3,2,0:T(8,128)(2,1)} %get-tuple-element.494, s32[]{:T(128)S(6)} %copy.116, f32[4,512,512]{1,2,0:T(8,128)} %subtract_exponential_fusion.3, f32[4,512,512]{1,2,0:T(8,128)} %fusion.230, bf16[1024,1,4,64]{0,3,2,1:T(8,128)(2,1)} %copy-done.4, s32[]{:T(128)S(6)} %select_n.231), kind=kOutput, calls=%fused_computation.41.clone.1 | convolution fusion | flops 139463168 | bytes 17563656 | tf_op jit(solution)/shard_map/while/body/eval_jaxpr/hqk,khc->qhc/dot_general | solution.py:122
  313.4 8.0 %fusion.232 = bf16[2,512,4,64]{1,3,2,0:T(8,128)(2,1)} fusion(bf16[2,512,4,64]{1,3,2,0:T(8,128)(2,1)} %get-tuple-element.495, s32[]{:T(128)S(6)} %copy.116, f32[4,512,512]{1,2,0:T(8,128)} %subtract_exponential_fusion.3, f32[4,512,512]{1,2,0:T(8,128)} %fusion.230, bf16[1024,1,4,64]{0,3,2,1:T(8,128)(2,1)} %copy-done.5, s32[]{:T(128)S(6)} %select_n.231), kind=kOutput, calls=%fused_computation.43.clone.1 | convolution fusion | flops 139463168 | bytes 17563656 | tf_op jit(solution)/shard_map/while/body/eval_jaxpr/hqk,qhc->khc/dot_general | solution.py:123
  321.3 8.1 %fusion.231 = bf16[2,512,4,64]{1,3,2,0:T(8,128)(2,1)} fusion(bf16[2,512,4,64]{1,3,2,0:T(8,128)(2,1)} %get-tuple-element.494, s32[]{:T(128)S(6)} %copy.116, f32[4,512,512]{1,2,0:T(8,128)} %subtract_exponential_fusion.3, f32[4,512,512]{1,2,0:T(8,128)} %fusion.230, bf16[1024,1,4,64]{0,3,2,1:T(8,128)(2,1)} %copy-done.4, s32[]{:T(128)S(6)} %select_n.231), kind=kOutput, calls=%fused_computation.41.clone.1 | convolution fusion | flops 139463168 | bytes 17563656 | tf_op jit(solution)/shard_map/while/body/eval_jaxpr/hqk,khc->qhc/dot_general | solution.py:122
  340.9 4.8 reshape.386
  347.1 4.8 reshape.387
  351.9 5.8 pad_maximum_fusion.2
  357.7 10.1 %gather_fusion.3 = bf16[1024,3,256]{2,1,0:T(4,128)(2,1)} fusion(bf16[1024,3,256]{2,1,0:T(4,128)(2,1)} %pad_maximum_fusion.2, s32[1024]{0:T(1024)S(1)} %copy-done.45), kind=kCustom, calls=%fused_computation.1.clone | custom fusion | bytes 3149824 | tf_op jit(solution)/shard_map/jit(_take)/gather | solution.py:311
  367.9 5.5 broadcast_select_fusion
  376.0 5.7 bitcast_convert_fusion
  390.4 60.9 %all-reduce.7.cloned.1.call-done = (bf16[128,3,256]{2,0,1:T(8,128)(2,1)}, bf16[256,128]{1,0:T(8,128)(2,1)}, bf16[128,1024]{1,0:T(8,128)(2,1)}, bf16[1024,128]{1,0:T(8,128)(2,1)}) async-done(((bf16[128,3,256]{2,0,1:T(8,128)(2,1)}, bf16[256,128]{1,0:T(8,128)(2,1)}, bf16[128,1024]{1,0:T(8,128)(2,1)}, bf16[1024,128]{1,0:T(8,128)(2,1)}), (bf16[128,3,256]{2,0,1:T(8,128)(2,1)}, bf16[256,128]{1,0:T(8,128)(2,1)}, ...) | async-done | bytes 786448 | tf_op jit(solution)/shard_map/psum | solution.py:335
  458.2 27.8 %reduce-scatter.11.cloned.1.call-done = bf16[256,1152]{1,0:T(8,128)(2,1)} async-done(((bf16[1024,1152]{1,0:T(8,128)(2,1)}), bf16[256,1152]{1,0:T(8,128)(2,1)}) %reduce-scatter.11.cloned.1.call-update) | async-done | bytes 589840 | tf_op jit(solution)/shard_map/reduce_scatter | solution.py:317
  493.2 135.2 %all-reduce.5.cloned.1.call-done = (f32[1024,128]{1,0:T(8,128)}, f32[128,1024]{1,0:T(8,128)}, f32[1024,128]{1,0:T(8,128)}, f32[128,1024]{1,0:T(8,128)}) async-done(((f32[1024,128]{1,0:T(8,128)}, f32[128,1024]{1,0:T(8,128)}, f32[1024,128]{1,0:T(8,128)}, f32[128,1024]{1,0:T(8,128)}), (f32[1024,128]{1,0:T(8,128)}, f32[128,1024]{1,0:T(8,128)}, f32[1024,128]{1,0:T(8,128)}, ...) | async-done | bytes 2097168 | tf_op jit(solution)/shard_map/psum | solution.py:330
  (316 shorter events, 144.7 us)
Async XLA Ops:
  7.2 160.0 %copy-start = (bf16[1024,128]{1,0:T(8,128)(2,1)S(1)}, bf16[1024,128]{1,0:T(8,128)(2,1)}, u32[]{:S(2)}) copy-start(bf16[1024,128]{1,0:T(8,128)(2,1)} %param.52) | copy-start | bytes 786436
  7.2 23.2 %copy-start.42 = (s32[1,1024]{1,0:T(1,128)S(1)}, s32[1,1024]{1,0:T(1,128)}, u32[]{:S(2)}) copy-start(s32[1,1024]{1,0:T(1,128)} %param.34) | copy-start | bytes 12292
  7.2 22.5 %copy-start.70 = (f32[2,256]{1,0:T(2,128)S(1)}, f32[2,256]{1,0:T(2,128)}, u32[]{:S(2)}) copy-start(f32[2,256]{1,0:T(2,128)} %param.39) | copy-start | bytes 6148
  7.2 31.7 %copy-start.73 = (bf16[1024,3,256]{2,0,1:T(8,128)(2,1)S(1)}, bf16[1024,3,256]{2,0,1:T(8,128)(2,1)}, u32[]{:S(2)}) copy-start(bf16[1024,3,256]{2,0,1:T(8,128)(2,1)} %param.38) | copy-start | bytes 4718596
  7.2 31.7 %all-gather.4.cloned.1.call-start = ((), (), s32[]{:S(2)}) async-start(), calls=%async_computation.4 | async-start | bytes 2621440 | tf_op jit(solution)/shard_map/all_gather | solution.py:217
  12.1 110.5 %reduce-scatter.5.cloned.1.call-start = ((), (), s32[]{:S(2)}) async-start(), calls=%async_computation.5 | async-start | bytes 2949120 | tf_op jit(solution)/shard_map/reduce_scatter | solution.py:228
  17.3 13.1 %copy-start.65 = (s32[128]{0:T(128)}, s32[128]{0:T(128)S(1)}, u32[]{:S(2)}) copy-start(s32[128]{0:T(128)S(1)} %and_select_fusion) | copy-start | bytes 1540
  29.7 12.6 %copy-start.18 = (bf16[1024,128]{1,0:T(8,128)(2,1)}, bf16[1024,128]{1,0:T(8,128)(2,1)S(1)}, u32[]{:S(2)}) copy-start(bf16[1024,128]{1,0:T(8,128)(2,1)S(1)} %all_gather.26) | copy-start | bytes 786436
  30.4 22.5 %copy-start.55 = (pred[1024]{0:T(1024)(128)(4,1)}, pred[1024]{0:T(1024)(128)(4,1)S(1)}, u32[]{:S(2)}) copy-start(pred[1024]{0:T(1024)(128)(4,1)S(1)} %compare_and_fusion) | copy-start | bytes 3076
  87.7 34.9 %copy-start.2 = (bf16[256,1024]{1,0:T(8,128)(2,1)S(1)}, bf16[256,1024]{1,0:T(8,128)(2,1)}, u32[]{:S(2)}) copy-start(bf16[256,1024]{1,0:T(8,128)(2,1)} %param.31) | copy-start | bytes 1572868
  89.4 83.9 %all-gather.6.cloned.1.call-start = ((), (), s32[]{:S(2)}) async-start(), calls=%async_computation.6 | async-start | bytes 2621440 | tf_op jit(solution)/shard_map/all_gather | solution.py:239
  126.3 102.2 %reduce-scatter.9.cloned.1.call-start = ((), (), s32[]{:S(2)}) async-start(), calls=%async_computation.8 | async-start | bytes 2949120 | tf_op jit(solution)/shard_map/reduce_scatter | solution.py:279
  130.3 27.2 %collective-permute-start = (bf16[256,1024]{1,0:T(8,128)(2,1)}, bf16[256,1024]{1,0:T(8,128)(2,1)}, u32[]{:S(2)}, u32[]{:S(2)}) collective-permute-start(bf16[256,1024]{1,0:T(8,128)(2,1)} %get-tuple-element.319), channel_id=1, source_target_pairs={{0,1},{1,2},{2,3},{3,0},{4,5},{5,6},{6,7},{7,4},{8,9},{9,10},{10,1... | collective-permute-start | bytes 1572872 | tf_op jit(solution)/shard_map/ppermute | solution.py:23
  130.4 33.1 %collective-permute-start.1 = (bf16[256,1024]{1,0:T(8,128)(2,1)}, bf16[256,1024]{1,0:T(8,128)(2,1)}, u32[]{:S(2)}, u32[]{:S(2)}) collective-permute-start(bf16[256,1024]{1,0:T(8,128)(2,1)} %get-tuple-element.319), channel_id=1, source_target_pairs={{0,3},{1,0},{2,1},{3,2},{4,7},{5,4},{6,5},{7,6},{8,11},{9,8},{10,9... | collective-permute-start | bytes 1572872 | tf_op jit(solution)/shard_map/ppermute | solution.py:28
  157.5 8.8 %collective-permute-start.2 = (bf16[256,1024]{1,0:T(8,128)(2,1)}, bf16[256,1024]{1,0:T(8,128)(2,1)S(1)}, u32[]{:S(2)}, u32[]{:S(2)}) collective-permute-start(bf16[256,1024]{1,0:T(8,128)(2,1)} %collective-permute-done), channel_id=1, source_target_pairs={{0,1},{1,2},{2,3},{3,0},{4,5},{5,6},{6,7},{7,4},{8,9},{9,10},{10,1... | collective-permute-start | bytes 1572872 | tf_op jit(solution)/shard_map/ppermute | solution.py:23
  194.5 35.2 %copy-start.47 = (f32[256]{0:T(256)S(1)}, f32[256]{0:T(256)}, u32[]{:S(2)}) copy-start(f32[256]{0:T(256)} %copy-done.46) | copy-start | bytes 3076
  194.5 35.2 %copy-start.48 = (f32[1024]{0:T(1024)S(1)}, f32[1024]{0:T(1024)}, u32[]{:S(2)}) copy-start(f32[1024]{0:T(1024)} %param.42) | copy-start | bytes 12292
  194.5 35.7 %copy-start.64 = (f32[256]{0:T(256)S(1)}, f32[256]{0:T(256)}, u32[]{:S(2)}) copy-start(f32[256]{0:T(256)} %copy-done.63) | copy-start | bytes 3076
  194.5 36.3 %copy-start.60 = (f32[256]{0:T(256)S(1)}, f32[256]{0:T(256)}, u32[]{:S(2)}) copy-start(f32[256]{0:T(256)} %copy-done.59) | copy-start | bytes 3076
  194.5 64.4 %all-gather.8.cloned.1.call-start = ((), (), s32[]{:S(2)}) async-start(), calls=%async_computation.9 | async-start | bytes 2621440 | tf_op jit(solution)/shard_map/all_gather | solution.py:296
  233.2 150.5 %reduce-scatter.7.cloned.1.call-start = ((), (), s32[]{:S(2)}) async-start(), calls=%async_computation.7 | async-start | bytes 2949120 | tf_op jit(solution)/shard_map/reduce_scatter | solution.py:248
  250.0 201.3 %all-reduce.7.cloned.1.call-start = ((), (), s32[]{:S(2)}) async-start(), calls=%async_computation.12 | async-start | bytes 1572864 | tf_op jit(solution)/shard_map/psum | solution.py:335
  375.9 110.1 %reduce-scatter.11.cloned.1.call-start = ((), (), s32[]{:S(2)}) async-start(), calls=%async_computation.10 | async-start | bytes 2949120 | tf_op jit(solution)/shard_map/reduce_scatter | solution.py:317
  381.7 246.6 %all-reduce.5.cloned.1.call-start = ((), (), s32[]{:S(2)}) async-start(), calls=%async_computation.11 | async-start | bytes 4194304 | tf_op jit(solution)/shard_map/psum | solution.py:330
  387.9 100.2 %copy-start.12 = (bf16[256,1024]{1,0:T(8,128)(2,1)S(1)}, bf16[256,1024]{1,0:T(8,128)(2,1)}, u32[]{:S(2)}) copy-start(bf16[256,1024]{1,0:T(8,128)(2,1)} %fusion.106) | copy-start | bytes 1572868
  454.5 34.9 %copy-start.3 = (bf16[256,1024]{1,0:T(8,128)(2,1)S(1)}, bf16[256,1024]{1,0:T(8,128)(2,1)}, u32[]{:S(2)}) copy-start(bf16[256,1024]{1,0:T(8,128)(2,1)} %param.31) | copy-start | bytes 1572868
  454.5 34.9 %copy-start.29 = (bf16[1024,128]{1,0:T(8,128)(2,1)S(1)}, bf16[1024,128]{1,0:T(8,128)(2,1)}, u32[]{:S(2)}) copy-start(bf16[1024,128]{1,0:T(8,128)(2,1)} %param.48) | copy-start | bytes 786436
  454.5 34.9 %copy-start.44 = (f32[256]{0:T(256)S(1)}, f32[256]{0:T(256)}, u32[]{:S(2)}) copy-start(f32[256]{0:T(256)} %copy-done.43) | copy-start | bytes 3076
  454.5 34.9 %copy-start.49 = (f32[1024]{0:T(1024)S(1)}, f32[1024]{0:T(1024)}, u32[]{:S(2)}) copy-start(f32[1024]{0:T(1024)} %param.36) | copy-start | bytes 12292
  458.2 33.1 %copy-start.62 = (f32[256]{0:T(256)S(1)}, f32[256]{0:T(256)}, u32[]{:S(2)}) copy-start(f32[256]{0:T(256)} %copy-done.61) | copy-start | bytes 3076
  458.2 33.1 %copy-start.53 = (f32[256]{0:T(256)S(1)}, f32[256]{0:T(256)}, u32[]{:S(2)}) copy-start(f32[256]{0:T(256)} %copy-done.52) | copy-start | bytes 3076
  491.7 143.1 %copy-start.1 = (bf16[1024,128]{1,0:T(8,128)(2,1)S(1)}, bf16[1024,128]{1,0:T(8,128)(2,1)}, u32[]{:S(2)}) copy-start(bf16[1024,128]{1,0:T(8,128)(2,1)} %param.52) | copy-start | bytes 786436
  (61 other events, 291.9 us)
Sparse Core Ops, SparseCore 0:
  12.2 26.6 all-gather.3
  89.5 33.0 reduce-scatter.4
  126.4 32.5 all-gather.5
  194.6 33.8 reduce-scatter.8
  233.3 23.4 all-gather.7
  259.3 33.1 reduce-scatter.6
  376.0 75.2 all-reduce.6
  453.8 32.0 reduce-scatter.10
  493.7 134.5 all-reduce.4
